TPU v7x, 512 devices: a whole 4x4x16 slice. The times are simulated.
512 devices in a mesh: space: 16 (over y, x_hi, core), date: 32 (over x_lo, z).
Axes of the slice: x: 4 (x_hi: 2, x_lo: 2; x = x_hi * 2 + x_lo), y: 4, z: 16, core: 2. Of those that a mesh axis runs over, the one named last changes fastest.
Arguments:
- obs: bfloat16 [7, 768, 128, 512], P(None, 'date', 'space'), may hold values from -30 to 30
- valid: int32 [768, 128, 512], P('date', 'space'), may hold values from 0 to 1
- days: int32 [768], P('date'), may hold values from 0 to 3649, as said below
Outputs:
- coefficients: float32 [7, 8, 128, 512], P(None, None, 'space', 'date')
- noise_scale: float32 [128, 512], P('space', 'date')
Inputs may be any that keep to these rules, and one draw needn't show every extreme that they name: `days`: day numbers of the acquisitions, in no particular order.
All inputs are finite; a program needn't handle non-finite values.
Results may differ from a plain program's by a relative error of at most 0.0003.
Values may be sent and summed in bfloat16 or wider, within the bound.
A program may use at most 128 MiB of HBM per device.

v0:
```python
import math
import jax
import jax.numpy as jnp
import numpy as np
from jax import lax
from jax.sharding import PartitionSpec as P

ITERS = 2
tukey_const = 4.685
ridge_value = 1.0
scale_eps = 1e-06
highest = lax.Precision.HIGHEST
pair_first = np.array(
    [row_index for row_index in range(8) for col_index in range(row_index, 8)], dtype=np.int32
)
pair_second = np.array(
    [col_index for row_index in range(8) for col_index in range(row_index, 8)], dtype=np.int32
)


def padded_2(block, sides, width):
    for axis, dim in sides:
        count = lax.axis_size(axis)
        forward = [(i, i + 1) for i in range(count - 1)]
        backward = [(target, source) for source, target in forward]
        low = lax.ppermute(
            lax.slice_in_dim(block, block.shape[dim] - width, None, axis=dim), axis, forward
        )
        high = lax.ppermute(lax.slice_in_dim(block, 0, width, axis=dim), axis, backward)
        block = jnp.concatenate([low, block, high], axis=dim)
    return block


def design(day_numbers):
    day_float = day_numbers.astype(jnp.float32)
    columns = [jnp.ones_like(day_float), (day_float - 1825.0) / 1825.0]
    angle = day_float * (2.0 * math.pi / 365.25)
    for harmonic in range(1, 4):
        columns.append(jnp.cos(harmonic * angle))
        columns.append(jnp.sin(harmonic * angle))
    return jnp.stack(columns, axis=1)


def form_moments(design_rows, weighted, observed):
    products = design_rows[:, pair_first] * design_rows[:, pair_second]
    gram_terms = jnp.dot(
        products.T, weighted, precision=highest, preferred_element_type=jnp.float32
    )
    cross_terms = jnp.einsum(
        "dk,bdp->bkp",
        design_rows,
        weighted[None] * observed,
        precision=highest,
        preferred_element_type=jnp.float32,
    )
    return jnp.concatenate([gram_terms, cross_terms.reshape(-1, weighted.shape[1])], axis=0)


def solve_terms(summed, band_count):
    term_count = 8
    entries = {}
    position = 0
    for row_index in range(term_count):
        for col_index in range(row_index, term_count):
            entries[row_index, col_index] = summed[position]
            position += 1
    right_sides = summed[position:].reshape((band_count, term_count) + summed.shape[1:])
    lower_factor = {}
    for col_index in range(term_count):
        pivot_value = entries[col_index, col_index] + ridge_value
        for inner_index in range(col_index):
            pivot_value = (
                pivot_value
                - lower_factor[col_index, inner_index] * lower_factor[col_index, inner_index]
            )
        pivot_root = jnp.sqrt(pivot_value)
        lower_factor[col_index, col_index] = pivot_root
        for row_index in range(col_index + 1, term_count):
            entry_value = entries[col_index, row_index]
            for inner_index in range(col_index):
                entry_value = (
                    entry_value
                    - lower_factor[row_index, inner_index] * lower_factor[col_index, inner_index]
                )
            lower_factor[row_index, col_index] = entry_value / pivot_root
    forward = []
    for row_index in range(term_count):
        running = right_sides[:, row_index]
        for inner_index in range(row_index):
            running = running - lower_factor[row_index, inner_index][None] * forward[inner_index]
        forward.append(running / lower_factor[row_index, row_index][None])
    solved = [None] * term_count
    for row_index in reversed(range(term_count)):
        running = forward[row_index]
        for inner_index in range(row_index + 1, term_count):
            running = running - lower_factor[inner_index, row_index][None] * solved[inner_index]
        solved[row_index] = running / lower_factor[row_index, row_index][None]
    return (jnp.stack(solved, axis=1), entries[0, 0])


def residual_power(design_rows, observed, coefficient):
    fitted = jnp.einsum(
        "dk,bkp->bdp",
        design_rows,
        coefficient,
        precision=highest,
        preferred_element_type=jnp.float32,
    )
    misfit = observed - fitted
    return jnp.mean(misfit * misfit, axis=0)


def box_sum(padded, row_count, col_count):
    across = padded[0:row_count]
    for offset in range(1, 5):
        across = across + padded[offset : offset + row_count]
    window_sum = across[:, 0:col_count]
    for offset in range(1, 5):
        window_sum = window_sum + across[:, offset : offset + col_count]
    return window_sum


def window_counts(first_index, length, whole):
    global_index = first_index + jnp.arange(length, dtype=jnp.int32)
    return (jnp.minimum(global_index + 2, whole - 1) - jnp.maximum(global_index - 2, 0) + 1).astype(
        jnp.float32
    )


def spread_rows(spread, weight_total, row_count, col_count):
    full_spread = lax.psum(spread, "date")
    variance = full_spread / (1.0 + weight_total)
    padded = padded_2(variance.reshape(row_count, col_count), (("space", 0),), 2)
    return jnp.pad(padded, ((0, 0), (2, 2)))


def next_weight(resid_power, smooth, mask_float):
    scaled = jnp.minimum(
        resid_power / (tukey_const * tukey_const * (smooth[None] + scale_eps)), 1.0
    )
    return mask_float * (1.0 - scaled) * (1.0 - scaled)


def on_device(obs, valid, days):
    band_count, date_count, row_count, col_count = obs.shape
    date_devices = lax.axis_size("date")
    date_index = lax.axis_index("date")
    cols_local = col_count // date_devices
    row_first = lax.axis_index("space") * row_count
    grid_rows = row_count * lax.axis_size("space")
    pixels = row_count * col_count
    mask_float = valid.astype(jnp.float32).reshape(date_count, pixels)
    observed = obs.astype(jnp.float32).reshape(band_count, date_count, pixels)
    design_rows = design(days)
    col_first = 0
    slice_start = date_index * cols_local
    counts = (
        window_counts(row_first, row_count, grid_rows)[:, None]
        * window_counts(col_first, col_count, col_count)[None, :]
    )
    weighted = mask_float
    for step in range(ITERS):
        local_terms = form_moments(design_rows, weighted, observed)
        summed = lax.psum(local_terms, "date")
        coefficient, weight_total = solve_terms(summed, band_count)
        resid_power = residual_power(design_rows, observed, coefficient)
        spread = jnp.sum(weighted * resid_power, axis=0)
        padded = spread_rows(spread, weight_total, row_count, col_count)
        smooth = (box_sum(padded, row_count, col_count) / counts).reshape(pixels)
        if step + 1 < ITERS:
            weighted = next_weight(resid_power, smooth, mask_float)
    coefficient = coefficient.reshape(band_count, 8, row_count, col_count)
    noise_scale = jnp.sqrt(smooth + scale_eps).reshape(row_count, col_count)
    coefficients = lax.dynamic_slice_in_dim(coefficient, slice_start, cols_local, 3)
    noise_block = lax.dynamic_slice_in_dim(noise_scale, slice_start, cols_local, 1)
    return (coefficients, noise_block)


def solution(mesh):
    in_specs = (P(None, "date", "space", None), P("date", "space", None), P("date"))
    out_specs = (P(None, None, "space", "date"), P("space", "date"))
    return jax.shard_map(
        on_device, mesh=mesh, in_specs=in_specs, out_specs=out_specs, check_vma=False
    )
```

profile of v0, /device:TPU:1, one launch (start us, length us, event | category | flops | bytes accessed | tf_op | source)
XLA Modules:
  0.0 877.3 jit_solution(6437620720839090686)
XLA Ops:
  11.1 2.4 reshape.5086
  17.9 245.5 %all-reduce.5.cloned.1.call-done = f32[92,4096]{1,0:T(8,128)} async-done(((f32[92,4096]{1,0:T(8,128)}), f32[92,4096]{1,0:T(8,128)}) %all-reduce.5.cloned.1.call-update) | async-done | bytes 1507344 | tf_op jit(solution)/shard_map/psum | solution.py:164
  263.4 2.4 slice_add_fusion.28
  265.7 1.8 subtract_sqrt_fusion.11
  267.6 1.7 subtract_sqrt_fusion.10
  272.4 2.0 subtract_divide_fusion.19
  274.4 3.7 subtract_divide_fusion.11
  278.1 3.7 stack.72
  281.8 3.8 fusion.6
  287.9 93.7 %psum.29 = f32[4096]{0:T(1024)} all-reduce(f32[4096]{0:T(1024)} %bitcast.399), channel_id=1, replica_groups=mesh['space'=16,'date'=32] {'date'}, use_global_device_ids=true, to_apply=%region_3.0 | all-reduce | flops 4096 | bytes 32768 | tf_op jit(solution)/shard_map/psum | solution.py:131
  383.6 54.4 %collective-permute-start = (f32[2,512]{1,0:T(2,128)}, f32[2,512]{1,0:T(2,128)S(1)}, u32[]{:S(2)}, u32[]{:S(2)}) collective-permute-start(f32[2,512]{1,0:T(2,128)} %slice.432), channel_id=1, source_target_pairs={{0,32},{32,64},{64,96},{96,128},{128,160},{160,192},{192,224},{224... | collective-permute-start | bytes 12296 | tf_op jit(solution)/shard_map/ppermute | solution.py:26
  438.5 2.1 collective-permute-start.1
  442.5 2.6 collective-permute-done.1
  451.6 231.3 %all-reduce.7.cloned.1.call-done = f32[92,4096]{1,0:T(8,128)} async-done(((f32[92,4096]{1,0:T(8,128)}), f32[92,4096]{1,0:T(8,128)}) %all-reduce.7.cloned.1.call-update) | async-done | bytes 1507344 | tf_op jit(solution)/shard_map/psum | solution.py:164
  682.9 1.8 slice_add_fusion.16
  684.7 1.9 subtract_sqrt_fusion.5
  691.3 3.8 fusion.144
  703.6 2.1 fusion.154
  705.7 3.6 stack.82
  709.3 3.8 fusion.7
  714.4 93.7 %psum.31 = f32[4096]{0:T(1024)S(1)} all-reduce(f32[4096]{0:T(1024)S(1)} %bitcast.400), channel_id=1, replica_groups=mesh['space'=16,'date'=32] {'date'}, use_global_device_ids=true, to_apply=%region_7.8 | all-reduce | flops 4096 | bytes 32768 | tf_op jit(solution)/shard_map/psum | solution.py:131
  808.1 54.4 %collective-permute-start.2 = (f32[2,512]{1,0:T(2,128)S(1)}, f32[2,512]{1,0:T(2,128)S(1)}, u32[]{:S(2)}, u32[]{:S(2)}) collective-permute-start(f32[2,512]{1,0:T(2,128)S(1)} %slice.491), channel_id=1, source_target_pairs={{0,32},{32,64},{64,96},{96,128},{128,160},{160,192},{192,224},{224... | collective-permute-start | bytes 12296 | tf_op jit(solution)/shard_map/ppermute | solution.py:26
  862.5 1.9 collective-permute-start.3
  865.9 3.0 collective-permute-done.3
  (124 shorter events, 41.7 us)
Async XLA Ops:
  7.2 256.2 %all-reduce.5.cloned.1.call-start = ((), (), s32[]{:S(2)}) async-start(), calls=%async_computation | async-start | bytes 3145728 | tf_op jit(solution)/shard_map/psum | solution.py:164
  17.6 665.3 %all-reduce.7.cloned.1.call-start = ((), (), s32[]{:S(2)}) async-start(), calls=%async_computation.1 | async-start | bytes 3145728 | tf_op jit(solution)/shard_map/psum | solution.py:164
  263.4 7.5 copy-start.5
  285.6 1.0 copy-start
  286.6 0.8 copy-start.2
  382.4 0.6 copy-start.19
  383.6 59.0 %collective-permute-start = (f32[2,512]{1,0:T(2,128)}, f32[2,512]{1,0:T(2,128)S(1)}, u32[]{:S(2)}, u32[]{:S(2)}) collective-permute-start(f32[2,512]{1,0:T(2,128)} %slice.432), channel_id=1, source_target_pairs={{0,32},{32,64},{64,96},{96,128},{128,160},{160,192},{192,224},{224... | collective-permute-start | bytes 12296 | tf_op jit(solution)/shard_map/ppermute | solution.py:26
  438.5 6.6 collective-permute-start.1
  448.0 1.6 copy-start.16
  682.9 7.0 copy-start.4
  702.9 0.6 copy-start.6
  713.1 1.0 copy-start.1
  713.1 1.1 copy-start.3
  713.1 1.1 copy-start.18
  713.1 151.3 %copy-start.11 = (f32[7,4096]{1,0:T(8,128)S(1)}, f32[7,4096]{1,0:T(8,128)}, u32[]{:S(2)}) copy-start(f32[7,4096]{1,0:T(8,128)} %get-tuple-element.23) | copy-start | bytes 344068
  713.1 151.4 %copy-start.10 = (f32[7,4096]{1,0:T(8,128)S(1)}, f32[7,4096]{1,0:T(8,128)}, u32[]{:S(2)}) copy-start(f32[7,4096]{1,0:T(8,128)} %get-tuple-element.21) | copy-start | bytes 344068
  713.1 151.4 %copy-start.14 = (f32[7,4096]{1,0:T(8,128)S(1)}, f32[7,4096]{1,0:T(8,128)}, u32[]{:S(2)}) copy-start(f32[7,4096]{1,0:T(8,128)} %get-tuple-element.19) | copy-start | bytes 344068
  713.2 151.5 %copy-start.9 = (f32[7,4096]{1,0:T(8,128)S(1)}, f32[7,4096]{1,0:T(8,128)}, u32[]{:S(2)}) copy-start(f32[7,4096]{1,0:T(8,128)} %get-tuple-element.17) | copy-start | bytes 344068
  713.2 151.5 %copy-start.13 = (f32[7,4096]{1,0:T(8,128)S(1)}, f32[7,4096]{1,0:T(8,128)}, u32[]{:S(2)}) copy-start(f32[7,4096]{1,0:T(8,128)} %get-tuple-element.15) | copy-start | bytes 344068
  713.2 151.6 %copy-start.8 = (f32[7,4096]{1,0:T(8,128)S(1)}, f32[7,4096]{1,0:T(8,128)}, u32[]{:S(2)}) copy-start(f32[7,4096]{1,0:T(8,128)} %get-tuple-element.13) | copy-start | bytes 344068
  714.2 150.7 %copy-start.12 = (f32[7,4096]{1,0:T(8,128)S(1)}, f32[7,4096]{1,0:T(8,128)}, u32[]{:S(2)}) copy-start(f32[7,4096]{1,0:T(8,128)} %get-tuple-element.11) | copy-start | bytes 344068
  714.2 150.8 %copy-start.7 = (f32[7,4096]{1,0:T(8,128)S(1)}, f32[7,4096]{1,0:T(8,128)}, u32[]{:S(2)}) copy-start(f32[7,4096]{1,0:T(8,128)} %get-tuple-element.2) | copy-start | bytes 344068
  808.1 57.9 %collective-permute-start.2 = (f32[2,512]{1,0:T(2,128)S(1)}, f32[2,512]{1,0:T(2,128)S(1)}, u32[]{:S(2)}, u32[]{:S(2)}) collective-permute-start(f32[2,512]{1,0:T(2,128)S(1)} %slice.491), channel_id=1, source_target_pairs={{0,32},{32,64},{64,96},{96,128},{128,160},{160,192},{192,224},{224... | collective-permute-start | bytes 12296 | tf_op jit(solution)/shard_map/ppermute | solution.py:26
  862.5 6.4 collective-permute-start.3
  (2 other events, 1.2 us)
Sparse Core Ops, SparseCore 0:
  17.7 245.5 all-reduce.4
  451.7 231.1 all-reduce.6
where the time goes:
time: 879 us; the launch traced here: 877 us
  waiting for transfers between devices  482 us (55%)
  blocking collectives  187 us (21%)
  starting transfers between devices  113 us (13%)
  other arithmetic  46.9 us (5%)
  local copies, waits for them, and re-layouts  20.9 us (2%)
  between operations  14.6 us (2%)
  matrix products  12 us (1%)
    psum x2, waiting for transfers between devices, on_device(): summed = lax.psum(local_terms, 'date')  477 us
    psum x2, blocking collectives, spread_rows(): full_spread = lax.psum(spread, 'date')  187 us
    ppermute x2, starting transfers between devices, padded_2(): lax.ppermute(lax.slice_in_dim(block, block.shape[dim] - width, None, axis...  109 us
  transfers between devices with their start and end apart: 6, of which 4 were waited for; matrix products, arithmetic and copies ran while one was open for 0% of the time, Pallas kernels for 0%

commit v1 on v0

--- a/solution.py
+++ b/solution.py
@@ -161,7 +161,7 @@
     weighted = mask_float
     for step in range(ITERS):
         local_terms = form_moments(design_rows, weighted, observed)
-        summed = lax.psum(local_terms, "date")
+        summed = jnp.sum(lax.all_gather(local_terms, "date"), axis=0)
         coefficient, weight_total = solve_terms(summed, band_count)
         resid_power = residual_power(design_rows, observed, coefficient)
         spread = jnp.sum(weighted * resid_power, axis=0)

time: 879 us -> 1480 us (1.68)
  waiting for transfers between devices: 482 us -> 1090 us
  other arithmetic: 46.9 us -> 91 us
  starting transfers between devices: 113 us -> 70.2 us
    all_gather x0 -> x2, waiting for transfers between devices: none -> 1090 us  [on_device(): summed = jnp.sum(lax.all_gather(local_terms, 'date'), axis=0)]
    psum x2 -> x0, waiting for transfers between devices: 477 us -> none  [on_device(): summed = lax.psum(local_terms, 'date')]
    ppermute x2, starting transfers between devices: 109 us -> 8.64 us  [padded_2(): lax.ppermute(lax.slice_in_dim(block, block.shape[dim] - width, None, axis...]
    ppermute x2, starting transfers between devices: 4.05 us -> 61.3 us  [padded_2(): lax.ppermute(lax.slice_in_dim(block, 0, width, axis=dim), axis, backward)]
    reduce_sum x0 -> x2, other arithmetic: none -> 37.3 us  [on_device(): summed = jnp.sum(lax.all_gather(local_terms, 'date'), axis=0)]
  transfers between devices with their start and end apart: 6 -> 6, of which waited for: 4 -> 2; matrix products, arithmetic and copies ran while one was open for 0% -> 0% of each run, Pallas kernels for 0% -> 0%
where the time goes in v1:
time: 1480 us
  waiting for transfers between devices  1090 us (74%)
  blocking collectives  183 us (12%)
  other arithmetic  91 us (6%)
  starting transfers between devices  70.2 us (5%)
  local copies, waits for them, and re-layouts  23.2 us (2%)
    all_gather x2, waiting for transfers between devices, on_device(): summed = jnp.sum(lax.all_gather(local_terms, 'date'), axis=0)  1090 us
    psum x2, blocking collectives, spread_rows(): full_spread = lax.psum(spread, 'date')  183 us
    ppermute x2, starting transfers between devices, padded_2(): lax.ppermute(lax.slice_in_dim(block, 0, width, axis=dim), axis, backward)  61.3 us
    reduce_sum x2, other arithmetic, on_device(): summed = jnp.sum(lax.all_gather(local_terms, 'date'), axis=0)  37.3 us
  transfers between devices with their start and end apart: 6, of which 2 were waited for; matrix products, arithmetic and copies ran while one was open for 0% of the time, Pallas kernels for 0%

profile of v1, /device:TPU:1, one launch (start us, length us, event | category | flops | bytes accessed | tf_op | source)
XLA Modules:
  0.0 1482.3 jit_solution(3241520964354738920)
XLA Ops:
  11.1 2.4 reshape.5086
  17.9 550.6 %all-gather.7.cloned.1.call-done = f32[32,92,4096]{2,1,0:T(8,128)} async-done(((f32[1,92,4096]{2,1,0:T(8,128)}), f32[32,92,4096]{2,1,0:T(8,128)}) %all-gather.7.cloned.1.call-update) | async-done | bytes 48234512 | tf_op jit(solution)/shard_map/all_gather | solution.py:164
  568.5 18.6 %reduce_sum.58 = f32[92,4096]{1,0:T(8,128)} reduce(f32[32,92,4096]{2,1,0:T(8,128)} %all-gather.7.cloned.1.call-done, f32[]{:T(128)} %constant.16.clone.1), dimensions={0}, to_apply=%region_0.0 | reduce | flops 11681792 | bytes 49741828 | tf_op jit(solution)/shard_map/reduce_sum | solution.py:164
  587.1 2.4 slice_add_fusion.28
  595.8 1.8 rsqrt_multiply_fusion.4
  598.7 1.8 sqrt_multiply_fusion.1
  600.8 2.0 subtract_divide_fusion.19
  602.8 3.7 subtract_divide_fusion.11
  606.5 3.6 stack.72
  610.1 3.8 fusion.6
  616.3 91.7 %psum.14 = f32[4096]{0:T(1024)} all-reduce(f32[4096]{0:T(1024)} %bitcast.403), channel_id=1, replica_groups=mesh['space'=16,'date'=32] {'date'}, use_global_device_ids=true, to_apply=%region_3.0 | all-reduce | flops 4096 | bytes 32768 | tf_op jit(solution)/shard_map/psum | solution.py:131
  710.6 30.7 %collective-permute-start.1 = (f32[2,512]{1,0:T(2,128)}, f32[2,512]{1,0:T(2,128)S(1)}, u32[]{:S(2)}, u32[]{:S(2)}) collective-permute-start(f32[2,512]{1,0:T(2,128)} %slice.434), channel_id=1, source_target_pairs={{32,0},{64,32},{96,64},{128,96},{160,128},{192,160},{224,192},{256... | collective-permute-start | bytes 12296 | tf_op jit(solution)/shard_map/ppermute | solution.py:29
  741.2 4.4 collective-permute-start
  754.7 536.5 %all-gather.9.cloned.1.call-done = f32[32,92,4096]{2,1,0:T(8,128)} async-done(((f32[1,92,4096]{2,1,0:T(8,128)}), f32[32,92,4096]{2,1,0:T(8,128)}) %all-gather.9.cloned.1.call-update) | async-done | bytes 48234512 | tf_op jit(solution)/shard_map/all_gather | solution.py:164
  1291.2 18.6 %reduce_sum.62 = f32[92,4096]{1,0:T(8,128)} reduce(f32[32,92,4096]{2,1,0:T(8,128)} %all-gather.9.cloned.1.call-done, f32[]{:T(128)} %constant.16.clone.1), dimensions={0}, to_apply=%region_4.5 | reduce | flops 11681792 | bytes 49741828 | tf_op jit(solution)/shard_map/reduce_sum | solution.py:164
  1309.9 1.8 slice_add_fusion.16
  1320.9 1.8 sqrt_multiply_fusion
  1323.0 3.5 fusion.144
  1335.0 2.1 fusion.154
  1337.1 3.5 stack.82
  1340.7 3.7 fusion.7
  1345.7 91.7 %psum.15 = f32[4096]{0:T(1024)S(1)} all-reduce(f32[4096]{0:T(1024)S(1)} %bitcast.404), channel_id=1, replica_groups=mesh['space'=16,'date'=32] {'date'}, use_global_device_ids=true, to_apply=%region_7.8 | all-reduce | flops 4096 | bytes 32768 | tf_op jit(solution)/shard_map/psum | solution.py:131
  1437.5 30.7 %collective-permute-start.3 = (f32[2,512]{1,0:T(2,128)S(1)}, f32[2,512]{1,0:T(2,128)S(1)}, u32[]{:S(2)}, u32[]{:S(2)}) collective-permute-start(f32[2,512]{1,0:T(2,128)S(1)} %slice.493), channel_id=1, source_target_pairs={{32,0},{64,32},{96,64},{128,96},{160,128},{192,160},{224,192},{256... | collective-permute-start | bytes 12296 | tf_op jit(solution)/shard_map/ppermute | solution.py:29
  1468.1 4.2 collective-permute-start.2
  (120 shorter events, 52.1 us)
Async XLA Ops:
  7.2 561.3 %all-gather.7.cloned.1.call-start = ((), (), s32[]{:S(2)}) async-start(), calls=%async_computation | async-start | bytes 51904512 | tf_op jit(solution)/shard_map/all_gather | solution.py:164
  13.5 0.6 copy-start.13
  17.6 1273.6 %all-gather.9.cloned.1.call-start = ((), (), s32[]{:S(2)}) async-start(), calls=%async_computation.1 | async-start | bytes 51904512 | tf_op jit(solution)/shard_map/all_gather | solution.py:164
  613.9 1.0 copy-start
  614.9 0.8 copy-start.2
  708.7 0.6 copy-start.16
  710.6 37.0 %collective-permute-start.1 = (f32[2,512]{1,0:T(2,128)}, f32[2,512]{1,0:T(2,128)S(1)}, u32[]{:S(2)}, u32[]{:S(2)}) collective-permute-start(f32[2,512]{1,0:T(2,128)} %slice.434), channel_id=1, source_target_pairs={{32,0},{64,32},{96,64},{128,96},{160,128},{192,160},{224,192},{256... | collective-permute-start | bytes 12296 | tf_op jit(solution)/shard_map/ppermute | solution.py:29
  741.2 6.4 collective-permute-start
  749.8 0.6 copy-start.14
  1334.4 0.6 copy-start.4
  1344.4 1.0 copy-start.1
  1344.4 1.1 copy-start.3
  1344.4 1.1 copy-start.15
  1344.4 127.9 %copy-start.9 = (f32[7,4096]{1,0:T(8,128)S(1)}, f32[7,4096]{1,0:T(8,128)}, u32[]{:S(2)}) copy-start(f32[7,4096]{1,0:T(8,128)} %get-tuple-element.23) | copy-start | bytes 344068
  1344.5 128.0 %copy-start.8 = (f32[7,4096]{1,0:T(8,128)S(1)}, f32[7,4096]{1,0:T(8,128)}, u32[]{:S(2)}) copy-start(f32[7,4096]{1,0:T(8,128)} %get-tuple-element.21) | copy-start | bytes 344068
  1344.5 128.1 %copy-start.12 = (f32[7,4096]{1,0:T(8,128)S(1)}, f32[7,4096]{1,0:T(8,128)}, u32[]{:S(2)}) copy-start(f32[7,4096]{1,0:T(8,128)} %get-tuple-element.19) | copy-start | bytes 344068
  1344.5 128.1 %copy-start.7 = (f32[7,4096]{1,0:T(8,128)S(1)}, f32[7,4096]{1,0:T(8,128)}, u32[]{:S(2)}) copy-start(f32[7,4096]{1,0:T(8,128)} %get-tuple-element.17) | copy-start | bytes 344068
  1344.5 128.2 %copy-start.11 = (f32[7,4096]{1,0:T(8,128)S(1)}, f32[7,4096]{1,0:T(8,128)}, u32[]{:S(2)}) copy-start(f32[7,4096]{1,0:T(8,128)} %get-tuple-element.15) | copy-start | bytes 344068
  1344.5 128.3 %copy-start.6 = (f32[7,4096]{1,0:T(8,128)S(1)}, f32[7,4096]{1,0:T(8,128)}, u32[]{:S(2)}) copy-start(f32[7,4096]{1,0:T(8,128)} %get-tuple-element.13) | copy-start | bytes 344068
  1345.5 127.3 %copy-start.10 = (f32[7,4096]{1,0:T(8,128)S(1)}, f32[7,4096]{1,0:T(8,128)}, u32[]{:S(2)}) copy-start(f32[7,4096]{1,0:T(8,128)} %get-tuple-element.11) | copy-start | bytes 344068
  1345.5 127.4 %copy-start.5 = (f32[7,4096]{1,0:T(8,128)S(1)}, f32[7,4096]{1,0:T(8,128)}, u32[]{:S(2)}) copy-start(f32[7,4096]{1,0:T(8,128)} %get-tuple-element.2) | copy-start | bytes 344068
  1437.5 36.4 %collective-permute-start.3 = (f32[2,512]{1,0:T(2,128)S(1)}, f32[2,512]{1,0:T(2,128)S(1)}, u32[]{:S(2)}, u32[]{:S(2)}) collective-permute-start(f32[2,512]{1,0:T(2,128)S(1)} %slice.493), channel_id=1, source_target_pairs={{32,0},{64,32},{96,64},{128,96},{160,128},{192,160},{224,192},{256... | collective-permute-start | bytes 12296 | tf_op jit(solution)/shard_map/ppermute | solution.py:29
  1468.1 5.8 collective-permute-start.2
Sparse Core Ops, SparseCore 0:
  17.7 550.7 all-gather.6
  754.9 536.3 all-gather.8
